TPU v7x, 512 devices: a whole 4x8x8 slice. The times are simulated.
512 devices in a mesh: dp: 32 (over x, z), tensor: 16 (over y, core).
Axes of the slice: x: 4, y: 8, z: 8, core: 2. Of those that a mesh axis runs over, the one named last changes fastest.
Arguments:
- activations: bfloat16 [16384, 16384], P('dp', 'tensor'), may hold values from -40 to 40, as said below
- token_ids: int32 [16384], P('dp'), may hold values from 0 to 128004, as said below
- weight: bfloat16 [16384, 16384], P('dp', 'tensor'), may hold values from -6 to 6
- inv_chol: float32 [128, 128, 1024], P('tensor', 'dp'), may hold values from -1 to 2, as said below
- bit_widths: int32 [128], P('tensor'), may hold values from 2 to 8, as said below
Outputs:
- quantized: bfloat16 [16384, 16384], P('dp', 'tensor')
- gram_blocks: float32 [128, 128, 128], P('tensor', 'dp')
- block_errors: float32 [128, 4], replicated
Inputs may be any that keep to these rules, and one draw needn't show every extreme that they name: `token_ids`: id 128004 marks padding. In the d-th aligned block of 512 tokens (d = 0 .. 31), exactly 170 + d*342//31 tokens are not padding, at positions drawn from the seed; the last block has no padding. `bit_widths`: each entry is 2, 3, 4 or 8. `inv_chol`: row i of block b, with j = b mod (8), holds a positive entry at column j*128+i, arbitrary entries at columns from (j+1)*128 on, and zeros elsewhere. `activations`: finite values.
All inputs are finite; a program needn't handle non-finite values.
Results may differ from a plain program's by a relative error of at most 0.001.
Values sent between devices are 32-bit elements; how exact they have to be, the bound alone decides.
No kernel may reach another device: no remote copies, remote signals or barrier semaphores. Data moves between devices by JAX's collectives and lax.ppermute only.
A program may use at most 64 MiB of HBM per device.

v0:
```python
import jax
import jax.numpy as jnp
from jax import lax
from jax.experimental import pallas as pl
from jax.experimental.pallas import tpu as pltpu
from jax.sharding import Mesh, PartitionSpec as P

OUT = 16384
BLK = 128
PANEL = 1024
NB = 8
DP = 32
ROWS = BLK // DP
NX, NZ, NY, NC = 4, 8, 8, 2
NT = NY * NC
PAIRS = [(j, c) for j in range(NB) for c in range(j + 1, NB)]
NP = len(PAIRS) + 1
HB = NB // 2
GT = HB + 1
PAD = 128004
LEVELS = (2.0, 4.0, 8.0, 128.0)

SIN = (
    0.9999996039231652,
    -6.579691570100355,
    12.986436001995736,
    -12.188101551479916,
    6.558042314696102,
    -1.9530321174789678,
)


def sine_over_two_pi(u):
    r = u - jnp.round(u)
    z = r * r
    p = SIN[-1] * z + SIN[-2]
    for a in SIN[-3::-1]:
        p = p * z + a
    return p * r


def params(*semantics):
    return pltpu.CompilerParams(dimension_semantics=semantics, vmem_limit_bytes=56 << 20)


def gram_kernel(x_ref, tok_ref, a_ref, *refs):
    outs, o_ref = refs[:NX], refs[NX]
    live = jnp.where(tok_ref[...] != PAD, 1.0, 0.0).astype(jnp.bfloat16)
    row = lax.broadcasted_iota(jnp.int32, (BLK, BLK), 0)
    col = lax.broadcasted_iota(jnp.int32, (BLK, BLK), 1)
    diag = jnp.zeros((BLK, BLK), jnp.float32)

    def gram(b):
        x = a_ref[:, b * BLK : (b + 1) * BLK]
        return jnp.dot(x.T * live, x, preferred_element_type=jnp.float32)

    def put(g, tile):
        for d in range(DP):
            o_ref[d // NZ, d % NZ, tile] = g[d * ROWS : (d + 1) * ROWS]

    for b in range(HB):
        lower = gram(b + HB)
        put(jnp.where(col >= row, gram(b), lower), b)
        value = jnp.sum(jnp.where(col == row, lower, 0.0), axis=1, keepdims=True)
        diag = jnp.where(col == b + HB, value, diag)
    put(diag, HB)
    for off in range(NX):
        outs[off][...] = o_ref[lax.rem(x_ref[0] + off, NX)]


def gram_partial(x, tokens, activations):
    vmem = pl.BlockSpec(memory_space=pltpu.VMEM)
    return pl.pallas_call(
        gram_kernel,
        out_shape=[jax.ShapeDtypeStruct((NZ, GT, ROWS, BLK), jnp.float32)] * NX,
        in_specs=[pl.BlockSpec(memory_space=pltpu.SMEM), vmem, vmem],
        out_specs=[vmem] * NX,
        scratch_shapes=[pltpu.VMEM((NX, NZ, GT, ROWS, BLK), jnp.float32)],
        compiler_params=params(),
        name="gram_partial",
    )(x, tokens, activations)


def pack_kernel(first_ref, f_ref, o_ref):
    lane = lax.broadcasted_iota(jnp.int32, (ROWS, BLK), 1)
    row = lax.broadcasted_iota(jnp.int32, (ROWS, BLK), 0)
    on_diag = lane == row + first_ref[0]
    diag = jnp.zeros((ROWS, BLK), jnp.float32)
    for j in range(NB):
        tile = f_ref[j, :, j * BLK : (j + 1) * BLK]
        value = jnp.sum(jnp.where(on_diag, tile, 0.0), axis=1, keepdims=True)
        diag = jnp.where(lane == j, value, diag)
    for i in range(NZ):
        o_ref[i, NP - 1] = diag
    for p, (j, c) in enumerate(PAIRS):
        tile = f_ref[j, :, c * BLK : (c + 1) * BLK]
        for i in range(NZ):
            o_ref[i, p] = tile


def pack(first, factor):
    vmem = pl.BlockSpec(memory_space=pltpu.VMEM)
    return pl.pallas_call(
        pack_kernel,
        out_shape=jax.ShapeDtypeStruct((NZ, NP, ROWS, BLK), jnp.float32),
        in_specs=[pl.BlockSpec(memory_space=pltpu.SMEM), vmem],
        out_specs=vmem,
        compiler_params=params(),
        name="pack",
    )(first, factor)


def sum_x_kernel(a_ref, b_ref, c_ref, d_ref, o_ref):
    o_ref[...] = (a_ref[...] + b_ref[...]) + (c_ref[...] + d_ref[...])


def sum_x(parts):
    vmem = pl.BlockSpec(memory_space=pltpu.VMEM)
    return pl.pallas_call(
        sum_x_kernel,
        out_shape=jax.ShapeDtypeStruct((NZ, GT, ROWS, BLK), jnp.float32),
        in_specs=[vmem] * NX,
        out_specs=vmem,
        compiler_params=params(),
        name="sum_x",
    )(*parts)


def sum_z_kernel(g_ref, own_ref, o_ref):
    total = g_ref[0]
    for i in range(1, NZ):
        total = total + g_ref[i]
    own_ref[...] = total
    for d in range(DP):
        o_ref[d] = total


def sum_z(received):
    vmem = pl.BlockSpec(memory_space=pltpu.VMEM)
    return pl.pallas_call(
        sum_z_kernel,
        out_shape=(
            pltpu.VMEM((GT, ROWS, BLK), jnp.float32),
            jax.ShapeDtypeStruct((DP, GT, ROWS, BLK), jnp.float32),
        ),
        in_specs=[vmem],
        out_specs=(vmem, vmem),
        compiler_params=params(),
        name="sum_z",
    )(received)


def error_kernel(w_ref, o_ref, d_ref):
    b = pl.program_id(0)
    row = lax.broadcasted_iota(jnp.int32, (BLK, BLK), 0)
    col = lax.broadcasted_iota(jnp.int32, (BLK, BLK), 1)
    upper = jnp.where(col > row, 2.0, jnp.where(col == row, 1.0, 0.0))
    lower = jnp.where(col < row, 2.0, 0.0)
    weight = jnp.where(b < HB, upper, lower)
    w = w_ref[...].astype(jnp.float32)
    bound = jnp.max(jnp.abs(w), axis=1, keepdims=True) + 1e-6
    unit = w * (1.0 / bound)
    for k, levels in enumerate(LEVELS):
        u = unit * (levels - 0.5)
        smooth = jnp.clip(u - sine_over_two_pi(u), -levels, levels - 1.0)
        e = (w - (bound * (1.0 / (levels - 0.5))) * smooth).astype(jnp.bfloat16)
        s = lax.dot_general(e, e, (((0,), (0,)), ((), ())), preferred_element_type=jnp.float32)
        value = jnp.sum(jnp.where(col == row, s, 0.0), axis=1, keepdims=True)
        diag = jnp.where((col == b) & (b >= HB), value, 0.0)
        s = s * weight
        for d in range(DP):
            part = slice(d * ROWS, (d + 1) * ROWS)
            o_ref[0, k, d] = s[part]
            before = jnp.where(b == 0, 0.0, d_ref[k, d])
            d_ref[k, d] = before + diag[part]


def error_grams(weight):
    rows = weight.shape[0]
    return pl.pallas_call(
        error_kernel,
        out_shape=(
            jax.ShapeDtypeStruct((NB, 4, DP, ROWS, BLK), jnp.float32),
            jax.ShapeDtypeStruct((4, DP, ROWS, BLK), jnp.float32),
        ),
        grid=(NB,),
        in_specs=[pl.BlockSpec((rows, BLK), lambda b: (0, b))],
        out_specs=(
            pl.BlockSpec((1, 4, DP, ROWS, BLK), lambda b: (b, 0, 0, 0, 0)),
            pl.BlockSpec((4, DP, ROWS, BLK), lambda b: (0, 0, 0, 0)),
        ),
        compiler_params=params("arbitrary"),
        name="error_grams",
    )(weight)


def score_kernel(tok_ref, g_ref, s_ref, d_ref, o_ref, row_ref):
    row_ref[...] = jnp.zeros((BLK, BLK), jnp.float32)
    live = jnp.where(tok_ref[...] != PAD, 1.0, 0.0)
    row_ref[4 * NB : 4 * NB + 1, :] = sum(live[:, i : i + BLK] for i in range(0, live.shape[1], BLK))
    diagonals = jnp.zeros((1, BLK), jnp.float32)
    for k in range(4):
        for b in range(NB):
            acc = g_ref[0, b % HB] * s_ref[b, k, 0]
            for d in range(1, DP):
                acc = acc + g_ref[d, b % HB] * s_ref[b, k, d]
            row_ref[k * NB + b : k * NB + b + 1, :] = jnp.sum(acc, axis=0, keepdims=True)
        acc = g_ref[0, HB] * d_ref[k, 0]
        for d in range(1, DP):
            acc = acc + g_ref[d, HB] * d_ref[k, d]
        acc = jnp.sum(acc, axis=0, keepdims=True)
        diagonals = diagonals + (pltpu.roll(acc, k * NB, 1) if k else acc)
    row = jnp.sum(row_ref[...].T, axis=0, keepdims=True) + diagonals
    for d in range(DP):
        o_ref[d] = row


def scores(tokens, gram, grams, diagonals):
    vmem = pl.BlockSpec(memory_space=pltpu.VMEM)
    return pl.pallas_call(
        score_kernel,
        out_shape=jax.ShapeDtypeStruct((DP, 1, BLK), jnp.float32),
        in_specs=[vmem] * 4,
        out_specs=vmem,
        scratch_shapes=[pltpu.VMEM((BLK, BLK), jnp.float32)],
        compiler_params=params(),
        name="scores",
    )(tokens, gram, grams, diagonals)


def rows_kernel(first_ref, g_ref, own_ref, o_ref):
    first = first_ref[0]
    lane = lax.broadcasted_iota(jnp.int32, (ROWS, BLK), 1)
    mine = lax.broadcasted_iota(jnp.int32, (ROWS, BLK), 0) + first
    pick = jnp.where(
        lax.broadcasted_iota(jnp.int32, (8, BLK), 1) == lax.broadcasted_iota(jnp.int32, (8, BLK), 0) + first, 1.0, 0.0
    )
    for b in range(HB):
        square = jnp.concatenate([g_ref[d, b] for d in range(DP)], axis=0)
        turned = lax.dot_general(
            pick,
            square,
            (((1,), (1,)), ((), ())),
            precision=lax.Precision.HIGHEST,
            preferred_element_type=jnp.float32,
        )[:ROWS]
        own = own_ref[b]
        diag = jnp.sum(jnp.where(lane == b + HB, own_ref[HB], 0.0), axis=1, keepdims=True)
        o_ref[b] = jnp.where(lane >= mine, own, turned)
        o_ref[b + HB] = jnp.where(lane < mine, own, jnp.where(lane == mine, diag, turned))


def gram_rows(first, gram, own):
    vmem = pl.BlockSpec(memory_space=pltpu.VMEM)
    return pl.pallas_call(
        rows_kernel,
        out_shape=pltpu.VMEM((NB, ROWS, BLK), jnp.float32),
        in_specs=[pl.BlockSpec(memory_space=pltpu.SMEM), vmem, vmem],
        out_specs=vmem,
        compiler_params=params(),
        name="gram_rows",
    )(first, gram, own)


def total_kernel(r_ref, own_ref, gram_ref, o_ref):
    row = r_ref[0]
    for d in range(1, DP):
        row = row + r_ref[d]
    lane = lax.broadcasted_iota(jnp.int32, (1, BLK), 1)
    count = jnp.sum(jnp.where(lane == 4 * NB, row, 0.0))
    gram_ref[...] = own_ref[...] / count
    scale = jnp.zeros((1, BLK), jnp.float32)
    for k, levels in enumerate(LEVELS):
        scale = jnp.where(lane // NB == k, levels * levels / (OUT * BLK), scale)
    row = row * scale / count
    for t in range(NT):
        o_ref[t] = row


def totals(rows, own):
    vmem = pl.BlockSpec(memory_space=pltpu.VMEM)
    return pl.pallas_call(
        total_kernel,
        out_shape=(
            jax.ShapeDtypeStruct((NB, ROWS, BLK), jnp.float32),
            jax.ShapeDtypeStruct((NT, 1, BLK), jnp.float32),
        ),
        in_specs=[vmem, vmem],
        out_specs=(vmem, vmem),
        compiler_params=params(),
        name="totals",
    )(rows, own)


def spread_kernel(r_ref, o_ref, row_ref):
    n = NT
    for t in range(n):
        row_ref[t : t + 1, :] = r_ref[t]
    lane = lax.broadcasted_iota(jnp.int32, (8, BLK), 1)
    source = lax.broadcasted_iota(jnp.int32, (8, BLK), 0)
    total = [jnp.zeros((1, BLK), jnp.float32)] * 4
    for h in range(n // 8):
        skewed = pltpu.roll(row_ref[h * 8 : (h + 1) * 8, :], 0, 1, stride=NB, stride_axis=0)
        for k in range(4):
            moved = pltpu.roll(skewed, (h * 8 * NB - k * NB) % BLK, 1)
            kept = jnp.where(lane // NB == source + h * 8, moved, 0.0)
            total[k] = total[k] + jnp.sum(kept, axis=0, keepdims=True)
    for k in range(4):
        o_ref[k : k + 1, :] = total[k]


def spread(rows):
    vmem = pl.BlockSpec(memory_space=pltpu.VMEM)
    return pl.pallas_call(
        spread_kernel,
        out_shape=jax.ShapeDtypeStruct((4, BLK), jnp.float32),
        in_specs=[vmem],
        out_specs=vmem,
        scratch_shapes=[pltpu.VMEM((NT, BLK), jnp.float32)],
        compiler_params=params(),
        name="spread",
    )(rows)


CHUNKS = 2


def quant_kernel(bits_ref, x_ref, w_ref, own_ref, left_ref, right_ref, far_ref, o_ref, c_ref, u_ref, slab_ref):
    rows = w_ref.shape[0] // CHUNKS
    x = x_ref[0]

    def slab(p):
        for off, ref in enumerate((own_ref, right_ref, far_ref, left_ref)):
            base = pl.multiple_of(lax.rem(x + off, NX) * (NZ * ROWS), NZ * ROWS)
            chunk = jnp.concatenate([ref[i, p] for i in range(NZ)], axis=0)
            slab_ref[pl.ds(base, NZ * ROWS), :] = chunk
        return slab_ref[...]

    inv_diag = 1.0 / slab(NP - 1)[:, :NB].T
    p = 0
    for j in range(NB):
        first = j * BLK
        width = PANEL - first - BLK
        if width:
            for i in range(width // BLK):
                u = slab(p)
                p += 1
                high = u.astype(jnp.bfloat16)
                low = (u - high.astype(jnp.float32)).astype(jnp.bfloat16)
                cols = slice(i * BLK, (i + 1) * BLK)
                u_ref[0:BLK, cols] = high
                u_ref[BLK : 2 * BLK, cols] = high
                u_ref[2 * BLK : 3 * BLK, cols] = low
        bits = bits_ref[j]
        levels = jnp.where(bits == 2, 2.0, jnp.where(bits == 3, 4.0, jnp.where(bits == 4, 8.0, 128.0)))
        half = levels - 0.5
        for h in range(CHUNKS):
            part = slice(h * rows, (h + 1) * rows)
            if j == 0:
                c = w_ref[part, :BLK].astype(jnp.float32)
            else:
                c = c_ref[part, first : first + BLK]
            step = (jnp.max(jnp.abs(c), axis=1, keepdims=True) + 1e-6) / half
            u = c * (1.0 / step)
            q = step * jnp.clip(u - sine_over_two_pi(u), -levels, levels - 1.0)
            o_ref[part, first : first + BLK] = q.astype(jnp.bfloat16)
            if width:
                e = (c - q) * inv_diag[j : j + 1, :]
                high = e.astype(jnp.bfloat16)
                low = (e - high.astype(jnp.float32)).astype(jnp.bfloat16)
                lhs = jnp.concatenate([high, low, high], axis=1)
                update = jnp.dot(lhs, u_ref[:, :width], preferred_element_type=jnp.float32)
                if j == 0:
                    rest = w_ref[part, BLK:].astype(jnp.float32)
                else:
                    rest = c_ref[part, first + BLK :]
                c_ref[part, first + BLK :] = rest - update


def quantize(bits, x, weight, factor):
    rows = weight.shape[0]
    return pl.pallas_call(
        quant_kernel,
        out_shape=jax.ShapeDtypeStruct((rows, PANEL), jnp.bfloat16),
        in_specs=[
            pl.BlockSpec(memory_space=pltpu.SMEM),
            pl.BlockSpec(memory_space=pltpu.SMEM),
        ]
        + [pl.BlockSpec(memory_space=pltpu.VMEM)] * 5,
        out_specs=pl.BlockSpec(memory_space=pltpu.VMEM),
        scratch_shapes=[
            pltpu.VMEM((rows, PANEL), jnp.float32),
            pltpu.VMEM((3 * BLK, PANEL - BLK), jnp.bfloat16),
            pltpu.VMEM((BLK, BLK), jnp.float32),
        ],
        compiler_params=params(),
        name="quantize",
    )(bits, x, weight, *factor)


def exchange(pieces, axes):
    return lax.all_to_all(pieces, axes, 0, 0, tiled=False)


def shift_x(piece, by):
    return lax.ppermute(piece, "x", [(i, (i + by) % NX) for i in range(NX)])


def near(array):
    return pltpu.with_memory_space_constraint(array, pltpu.VMEM)


def per_device(activations, token_ids, weight, inv_chol, bit_widths):
    dp = ("x", "z")
    tensor = ("y", "c")
    tokens = token_ids.reshape(1, -1)
    x = lax.axis_index("x").reshape(1).astype(jnp.int32)
    first = (lax.axis_index(dp) * ROWS).reshape(1).astype(jnp.int32)
    packed = pack(first, inv_chol)
    mine = exchange(packed, "z")
    partial = gram_partial(x, tokens, activations)
    parts = [near(partial[0])]
    for off in range(1, NX):
        parts.append(near(shift_x(partial[off], off)))
    rows = sum_x(parts)
    mine, rows = lax.optimization_barrier((mine, rows))
    rows = exchange(rows, "z")
    left = shift_x(mine, 1)
    right = shift_x(mine, -1)
    own, copies = sum_z(near(rows))
    gram = exchange(copies, dp)
    grams, diagonals = error_grams(weight)
    row = scores(tokens, near(gram), near(grams), diagonals)
    left_late, _ = lax.optimization_barrier((left, row))
    row = exchange(row, dp)
    far = shift_x(left_late, 1)
    rows = gram_rows(first, near(gram), near(own))
    quantized = quantize(bit_widths, x, weight, tuple(map(near, (mine, left, right, far))))
    gram_out, row = totals(near(row), near(rows))
    row = exchange(row, tensor)
    block_errors = spread(near(row))
    return quantized, gram_out, block_errors.T


def solution(mesh):
    fine = Mesh(mesh.devices.reshape(NX, NZ, NY, NC), ("x", "z", "y", "c"))
    dp = ("x", "z")
    tensor = ("y", "c")
    placed = (P(dp, tensor), P(dp), P(dp, tensor), P(tensor, dp, None), P(tensor))
    return jax.shard_map(
        per_device,
        mesh=fine,
        in_specs=placed,
        out_specs=(P(dp, tensor), P(tensor, dp, None), P()),
        check_vma=False,
    )
```

profile of v0, /device:TPU:1, one launch (start us, length us, event | category | flops | bytes accessed | tf_op | source)
XLA Modules:
  0.0 119.5 jit_solution(16503415725479059204)
XLA Ops:
  0.6 1.8 %pack.1 = f32[8,29,4,128]{3,2,1,0:T(4,128)} custom-call(s32[1]{0:T(128)} %bitcast.1.first_ref, f32[8,4,1024]{2,1,0:T(4,128)} %f_ref.1), custom_call_target="tpu_custom_call" | custom-call | tf_op jit(solution)/shard_map/pack/pallas_call | solution.py:103
  2.4 10.9 %all-to-all-start = ((f32[8,29,4,128]{3,2,1,0:T(4,128)}), f32[8,29,4,128]{3,2,1,0:T(4,128)S(1)}, u32[]{:S(2)}, u32[]{:S(2)}) async-start(f32[8,29,4,128]{3,2,1,0:T(4,128)} %pack.1), calls=%async_computation | async-start | bytes 950272 | tf_op jit(solution)/shard_map/all_to_all | solution.py:402
  13.3 2.5 %gram_partial.1 = (f32[8,5,4,128]{3,2,1,0:T(4,128)}, f32[8,5,4,128]{3,2,1,0:T(4,128)}, f32[8,5,4,128]{3,2,1,0:T(4,128)}, f32[8,5,4,128]{3,2,1,0:T(4,128)}) custom-call(s32[1]{0:T(128)} %bitcast.x_ref, s32[1,512]{1,0:T(1,128)} %bitcast.4, bf16[512,1024]{1,0:T(8,128)(2,1)} %a_ref.1), custom_call_target="tpu_custom_call" | custom-call | tf_op jit(solution)/shard_map/gram_partial/pallas_call | solution.py:73
  15.8 3.1 %collective-permute-start = (f32[8,5,4,128]{3,2,1,0:T(4,128)}, f32[8,5,4,128]{3,2,1,0:T(4,128)S(1)}, u32[]{:S(2)}, u32[]{:S(2)}) collective-permute-start(f32[8,5,4,128]{3,2,1,0:T(4,128)} %get-tuple-element.17), channel_id=1, source_target_pairs={{0,128},{128,256},{256,384},{384,0},{1,129},{129,257},{257,385},{3... | collective-permute-start | bytes 245768 | tf_op jit(solution)/shard_map/ppermute | solution.py:406
  18.9 4.4 %collective-permute-start.1 = (f32[8,5,4,128]{3,2,1,0:T(4,128)}, f32[8,5,4,128]{3,2,1,0:T(4,128)S(1)}, u32[]{:S(2)}, u32[]{:S(2)}) collective-permute-start(f32[8,5,4,128]{3,2,1,0:T(4,128)} %get-tuple-element.18), channel_id=1, source_target_pairs={{0,256},{128,384},{256,0},{384,128},{1,257},{129,385},{257,1},{385... | collective-permute-start | bytes 245768 | tf_op jit(solution)/shard_map/ppermute | solution.py:406
  23.3 3.1 %collective-permute-start.2 = (f32[8,5,4,128]{3,2,1,0:T(4,128)}, f32[8,5,4,128]{3,2,1,0:T(4,128)S(1)}, u32[]{:S(2)}, u32[]{:S(2)}) collective-permute-start(f32[8,5,4,128]{3,2,1,0:T(4,128)} %get-tuple-element.19), channel_id=1, source_target_pairs={{0,384},{128,0},{256,128},{384,256},{1,385},{129,1},{257,129},{385... | collective-permute-start | bytes 245768 | tf_op jit(solution)/shard_map/ppermute | solution.py:406
  26.4 0.0 collective-permute-done.b_ref
  26.4 0.0 collective-permute-done.1.c_ref
  26.4 2.6 %collective-permute-done.2.d_ref = f32[8,5,4,128]{3,2,1,0:T(4,128)S(1)} collective-permute-done((f32[8,5,4,128]{3,2,1,0:T(4,128)}, f32[8,5,4,128]{3,2,1,0:T(4,128)S(1)}, u32[]{:S(2)}, u32[]{:S(2)}) %collective-permute-start.2) | collective-permute-done | bytes 81952 | tf_op jit(solution)/shard_map/ppermute | solution.py:406
  29.0 0.9 copy-done.1
  29.9 0.7 sum_x.1
  30.5 0.0 all-to-all-done.own_ref
  30.5 13.8 %all_to_all.25.g_ref = f32[8,5,4,128]{3,2,1,0:T(4,128)S(1)} all-to-all(f32[8,5,4,128]{3,2,1,0:T(4,128)} %sum_x.1), channel_id=1, replica_groups=mesh['x'=4,'z'=8,'y'=8,'c'=2] {'z'}, dimensions={0} | all-to-all | bytes 163840 | tf_op jit(solution)/shard_map/all_to_all | solution.py:402
  44.3 0.8 sum_z.1
  45.1 4.0 %all-to-all-start.2 = ((f32[32,5,4,128]{3,2,1,0:T(4,128)}), f32[32,5,4,128]{3,2,1,0:T(4,128)S(1)}, u32[]{:S(2)}, u32[]{:S(2)}) async-start(f32[32,5,4,128]{3,2,1,0:T(4,128)} %get-tuple-element.22), calls=%async_computation.2 | async-start | bytes 655360 | tf_op jit(solution)/shard_map/all_to_all | solution.py:402
  49.1 3.1 %collective-permute-start.3 = (f32[8,29,4,128]{3,2,1,0:T(4,128)S(1)}, f32[8,29,4,128]{3,2,1,0:T(4,128)S(1)}, u32[]{:S(2)}, u32[]{:S(2)}) collective-permute-start(f32[8,29,4,128]{3,2,1,0:T(4,128)S(1)} %all-to-all-done.own_ref), channel_id=1, source_target_pairs={{0,128},{128,256},{256,384},{384,0},{1,129},{129,257},{257,385},{3... | collective-permute-start | bytes 1425416 | tf_op jit(solution)/shard_map/ppermute | solution.py:406
  52.3 11.2 %error_grams.1 = (f32[8,4,32,4,128]{4,3,2,1,0:T(4,128)}, f32[4,32,4,128]{3,2,1,0:T(4,128)}) custom-call(bf16[512,1024]{1,0:T(8,128)(2,1)} %w_ref.3), custom_call_target="tpu_custom_call" | custom-call | tf_op jit(solution)/shard_map/error_grams/pallas_call | solution.py:180
  63.4 3.3 %collective-permute-start.4 = (f32[8,29,4,128]{3,2,1,0:T(4,128)S(1)}, f32[8,29,4,128]{3,2,1,0:T(4,128)S(1)}, u32[]{:S(2)}, u32[]{:S(2)}) collective-permute-start(f32[8,29,4,128]{3,2,1,0:T(4,128)S(1)} %all-to-all-done.own_ref), channel_id=1, source_target_pairs={{0,384},{128,0},{256,128},{384,256},{1,385},{129,1},{257,129},{385... | collective-permute-start | bytes 1425416 | tf_op jit(solution)/shard_map/ppermute | solution.py:406
  66.8 0.0 all-to-all-done.2.g_ref
  66.8 1.6 %copy-done = f32[8,4,32,4,128]{4,3,2,1,0:T(4,128)S(1)} copy-done((f32[8,4,32,4,128]{4,3,2,1,0:T(4,128)S(1)}, f32[8,4,32,4,128]{4,3,2,1,0:T(4,128)}, u32[]{:S(2)}) %copy-start) | copy-done | bytes 2097176
  68.4 2.2 %scores.1 = f32[32,1,128]{2,1,0:T(1,128)} custom-call(s32[1,512]{1,0:T(1,128)} %bitcast.5, f32[32,5,4,128]{3,2,1,0:T(4,128)S(1)} %all-to-all-done.2.g_ref, f32[8,4,32,4,128]{4,3,2,1,0:T(4,128)S(1)} %copy-done, f32[4,32,4,128]{3,2,1,0:T(4,128)} %get-tuple-element.24.d_ref), custom_call_target="tpu_custom_call" | custom-call | tf_op jit(solution)/shard_map/scores/pallas_call | solution.py:220
  70.5 0.0 collective-permute-done.3.left_ref
  70.5 1.9 %collective-permute-start.5 = (f32[8,29,4,128]{3,2,1,0:T(4,128)S(1)}, f32[8,29,4,128]{3,2,1,0:T(4,128)S(1)}, u32[]{:S(2)}, u32[]{:S(2)}) collective-permute-start(f32[8,29,4,128]{3,2,1,0:T(4,128)S(1)} %collective-permute-done.3.left_ref), channel_id=1, source_target_pairs={{0,128},{128,256},{256,384},{384,0},{1,129},{129,257},{257,385},{3... | collective-permute-start | bytes 1425416 | tf_op jit(solution)/shard_map/ppermute | solution.py:406
  72.5 9.2 %all-to-all-start.3 = ((f32[32,1,128]{2,1,0:T(1,128)}), f32[32,1,128]{2,1,0:T(1,128)S(1)}, u32[]{:S(2)}, u32[]{:S(2)}) async-start(f32[32,1,128]{2,1,0:T(1,128)} %scores.1), calls=%async_computation.3 | async-start | bytes 32768 | tf_op jit(solution)/shard_map/all_to_all | solution.py:402
  81.7 0.5 gram_rows.1.own_ref
  82.2 8.1 %all-to-all-done.3.r_ref = f32[32,1,128]{2,1,0:T(1,128)S(1)} async-done(((f32[32,1,128]{2,1,0:T(1,128)}), f32[32,1,128]{2,1,0:T(1,128)S(1)}, u32[]{:S(2)}, u32[]{:S(2)}) %all-to-all-start.3) | async-done | bytes 16416 | tf_op jit(solution)/shard_map/all_to_all | solution.py:402
  90.3 0.8 totals.1
  91.0 21.3 %all_to_all.26.r_ref = f32[16,1,128]{2,1,0:T(1,128)S(1)} all-to-all(f32[16,1,128]{2,1,0:T(1,128)} %get-tuple-element.28), channel_id=1, replica_groups=mesh['x'=4,'z'=8,'y'=8,'c'=2] {'y','c'}, dimensions={0} | all-to-all | bytes 16384 | tf_op jit(solution)/shard_map/all_to_all | solution.py:402
  112.3 0.7 spread.1
  113.0 0.0 collective-permute-done.4.right_ref
  113.0 0.0 collective-permute-done.5.far_ref
  113.1 6.4 %quantize.1 = bf16[512,1024]{1,0:T(8,128)(2,1)} custom-call(s32[8]{0:T(128)} %bits_ref.1, s32[1]{0:T(128)} %bitcast.x_ref, bf16[512,1024]{1,0:T(8,128)(2,1)} %w_ref.3, f32[8,29,4,128]{3,2,1,0:T(4,128)S(1)} %all-to-all-done.own_ref, f32[8,29,4,128]{3,2,1,0:T(4,128)S(1)} %collective-permute-done.3.left_ref, ...), custom_call_target="tpu_custom_call" | custom-call | tf_op jit(solution)/shard_map/quantize/pallas_call | solution.py:382
  (2 shorter events, 0.0 us)
Async XLA Ops:
  2.4 28.1 %all-to-all-start = ((f32[8,29,4,128]{3,2,1,0:T(4,128)}), f32[8,29,4,128]{3,2,1,0:T(4,128)S(1)}, u32[]{:S(2)}, u32[]{:S(2)}) async-start(f32[8,29,4,128]{3,2,1,0:T(4,128)} %pack.1), calls=%async_computation | async-start | bytes 950272 | tf_op jit(solution)/shard_map/all_to_all | solution.py:402
  15.8 10.6 %collective-permute-start = (f32[8,5,4,128]{3,2,1,0:T(4,128)}, f32[8,5,4,128]{3,2,1,0:T(4,128)S(1)}, u32[]{:S(2)}, u32[]{:S(2)}) collective-permute-start(f32[8,5,4,128]{3,2,1,0:T(4,128)} %get-tuple-element.17), channel_id=1, source_target_pairs={{0,128},{128,256},{256,384},{384,0},{1,129},{129,257},{257,385},{3... | collective-permute-start | bytes 245768 | tf_op jit(solution)/shard_map/ppermute | solution.py:406
  18.9 7.4 %collective-permute-start.1 = (f32[8,5,4,128]{3,2,1,0:T(4,128)}, f32[8,5,4,128]{3,2,1,0:T(4,128)S(1)}, u32[]{:S(2)}, u32[]{:S(2)}) collective-permute-start(f32[8,5,4,128]{3,2,1,0:T(4,128)} %get-tuple-element.18), channel_id=1, source_target_pairs={{0,256},{128,384},{256,0},{384,128},{1,257},{129,385},{257,1},{385... | collective-permute-start | bytes 245768 | tf_op jit(solution)/shard_map/ppermute | solution.py:406
  23.3 5.7 %collective-permute-start.2 = (f32[8,5,4,128]{3,2,1,0:T(4,128)}, f32[8,5,4,128]{3,2,1,0:T(4,128)S(1)}, u32[]{:S(2)}, u32[]{:S(2)}) collective-permute-start(f32[8,5,4,128]{3,2,1,0:T(4,128)} %get-tuple-element.19), channel_id=1, source_target_pairs={{0,384},{128,0},{256,128},{384,256},{1,385},{129,1},{257,129},{385... | collective-permute-start | bytes 245768 | tf_op jit(solution)/shard_map/ppermute | solution.py:406
  29.0 0.9 copy-start.1
  45.1 21.7 %all-to-all-start.2 = ((f32[32,5,4,128]{3,2,1,0:T(4,128)}), f32[32,5,4,128]{3,2,1,0:T(4,128)S(1)}, u32[]{:S(2)}, u32[]{:S(2)}) async-start(f32[32,5,4,128]{3,2,1,0:T(4,128)} %get-tuple-element.22), calls=%async_computation.2 | async-start | bytes 655360 | tf_op jit(solution)/shard_map/all_to_all | solution.py:402
  49.1 21.4 %collective-permute-start.3 = (f32[8,29,4,128]{3,2,1,0:T(4,128)S(1)}, f32[8,29,4,128]{3,2,1,0:T(4,128)S(1)}, u32[]{:S(2)}, u32[]{:S(2)}) collective-permute-start(f32[8,29,4,128]{3,2,1,0:T(4,128)S(1)} %all-to-all-done.own_ref), channel_id=1, source_target_pairs={{0,128},{128,256},{256,384},{384,0},{1,129},{129,257},{257,385},{3... | collective-permute-start | bytes 1425416 | tf_op jit(solution)/shard_map/ppermute | solution.py:406
  63.4 49.6 %collective-permute-start.4 = (f32[8,29,4,128]{3,2,1,0:T(4,128)S(1)}, f32[8,29,4,128]{3,2,1,0:T(4,128)S(1)}, u32[]{:S(2)}, u32[]{:S(2)}) collective-permute-start(f32[8,29,4,128]{3,2,1,0:T(4,128)S(1)} %all-to-all-done.own_ref), channel_id=1, source_target_pairs={{0,384},{128,0},{256,128},{384,256},{1,385},{129,1},{257,129},{385... | collective-permute-start | bytes 1425416 | tf_op jit(solution)/shard_map/ppermute | solution.py:406
  66.8 1.6 %copy-start = (f32[8,4,32,4,128]{4,3,2,1,0:T(4,128)S(1)}, f32[8,4,32,4,128]{4,3,2,1,0:T(4,128)}, u32[]{:S(2)}) copy-start(f32[8,4,32,4,128]{4,3,2,1,0:T(4,128)} %get-tuple-element.23.s_ref) | copy-start | bytes 6291460
  70.5 42.5 %collective-permute-start.5 = (f32[8,29,4,128]{3,2,1,0:T(4,128)S(1)}, f32[8,29,4,128]{3,2,1,0:T(4,128)S(1)}, u32[]{:S(2)}, u32[]{:S(2)}) collective-permute-start(f32[8,29,4,128]{3,2,1,0:T(4,128)S(1)} %collective-permute-done.3.left_ref), channel_id=1, source_target_pairs={{0,128},{128,256},{256,384},{384,0},{1,129},{129,257},{257,385},{3... | collective-permute-start | bytes 1425416 | tf_op jit(solution)/shard_map/ppermute | solution.py:406
  72.5 17.8 %all-to-all-start.3 = ((f32[32,1,128]{2,1,0:T(1,128)}), f32[32,1,128]{2,1,0:T(1,128)S(1)}, u32[]{:S(2)}, u32[]{:S(2)}) async-start(f32[32,1,128]{2,1,0:T(1,128)} %scores.1), calls=%async_computation.3 | async-start | bytes 32768 | tf_op jit(solution)/shard_map/all_to_all | solution.py:402
where the time goes:
time: 120 us; the launch traced here: 119 us
  starting transfers between devices  43 us (36%)
  blocking collectives  35 us (29%)
  Pallas kernels  27.5 us (23%)
  waiting for transfers between devices  10.7 us (9%)
  local copies, waits for them, and re-layouts  2.47 us (2%)
    all_to_all x2, blocking collectives, exchange(): return lax.all_to_all(pieces, axes, 0, 0, tiled=False)  35 us
    all_to_all x3, starting transfers between devices, exchange(): return lax.all_to_all(pieces, axes, 0, 0, tiled=False)  24.1 us
    ppermute x6, starting transfers between devices, shift_x(): return lax.ppermute(piece, 'x', [(i, (i + by) % NX) for i in range(NX)])  18.9 us
    pallas_call x1, Pallas kernels, error_grams(): pl.pallas_call(error_kernel, out_shape=(jax.ShapeDtypeStruct((NB, 4, DP,...  11.2 us
    all_to_all x3, waiting for transfers between devices, exchange(): return lax.all_to_all(pieces, axes, 0, 0, tiled=False)  8.09 us
    pallas_call x1, Pallas kernels, quantize(): pl.pallas_call(quant_kernel, out_shape=jax.ShapeDtypeStruct((rows, PANEL)...  6.44 us
    ppermute x6, waiting for transfers between devices, shift_x(): return lax.ppermute(piece, 'x', [(i, (i + by) % NX) for i in range(NX)])  2.62 us
    pallas_call x1, Pallas kernels, gram_partial(): pl.pallas_call(gram_kernel, out_shape=[jax.ShapeDtypeStruct((NZ, GT, ROWS...  2.54 us
  transfers between devices with their start and end apart: 9, of which 2 were waited for; matrix products, arithmetic and copies ran while one was open for 0% of the time, Pallas kernels for 16%

commit v1 on v0

--- a/solution.py
+++ b/solution.py
@@ -43,8 +43,7 @@
     return pltpu.CompilerParams(dimension_semantics=semantics, vmem_limit_bytes=56 << 20)
 
 
-def gram_kernel(x_ref, tok_ref, a_ref, *refs):
-    outs, o_ref = refs[:NX], refs[NX]
+def gram_kernel(tok_ref, a_ref, o_ref):
     live = jnp.where(tok_ref[...] != PAD, 1.0, 0.0).astype(jnp.bfloat16)
     row = lax.broadcasted_iota(jnp.int32, (BLK, BLK), 0)
     col = lax.broadcasted_iota(jnp.int32, (BLK, BLK), 1)
@@ -64,24 +63,21 @@
         value = jnp.sum(jnp.where(col == row, lower, 0.0), axis=1, keepdims=True)
         diag = jnp.where(col == b + HB, value, diag)
     put(diag, HB)
-    for off in range(NX):
-        outs[off][...] = o_ref[lax.rem(x_ref[0] + off, NX)]
-
-
-def gram_partial(x, tokens, activations):
+
+
+def gram_partial(tokens, activations):
     vmem = pl.BlockSpec(memory_space=pltpu.VMEM)
     return pl.pallas_call(
         gram_kernel,
-        out_shape=[jax.ShapeDtypeStruct((NZ, GT, ROWS, BLK), jnp.float32)] * NX,
-        in_specs=[pl.BlockSpec(memory_space=pltpu.SMEM), vmem, vmem],
-        out_specs=[vmem] * NX,
-        scratch_shapes=[pltpu.VMEM((NX, NZ, GT, ROWS, BLK), jnp.float32)],
+        out_shape=pltpu.VMEM((NX, NZ, GT, ROWS, BLK), jnp.float32),
+        in_specs=[vmem, vmem],
+        out_specs=vmem,
         compiler_params=params(),
         name="gram_partial",
-    )(x, tokens, activations)
-
-
-def pack_kernel(first_ref, f_ref, o_ref):
+    )(tokens, activations)
+
+
+def sum_x_kernel(first_ref, f_ref, g_ref, o_ref):
     lane = lax.broadcasted_iota(jnp.int32, (ROWS, BLK), 1)
     row = lax.broadcasted_iota(jnp.int32, (ROWS, BLK), 0)
     on_diag = lane == row + first_ref[0]
@@ -96,40 +92,29 @@
         tile = f_ref[j, :, c * BLK : (c + 1) * BLK]
         for i in range(NZ):
             o_ref[i, p] = tile
-
-
-def pack(first, factor):
-    vmem = pl.BlockSpec(memory_space=pltpu.VMEM)
-    return pl.pallas_call(
-        pack_kernel,
-        out_shape=jax.ShapeDtypeStruct((NZ, NP, ROWS, BLK), jnp.float32),
-        in_specs=[pl.BlockSpec(memory_space=pltpu.SMEM), vmem],
+    for i in range(NZ):
+        total = g_ref[0, i]
+        for x in range(1, NX):
+            total = total + g_ref[x, i]
+        o_ref[i, NP:] = total
+
+
+def sum_x(first, factor, received):
+    vmem = pl.BlockSpec(memory_space=pltpu.VMEM)
+    return pl.pallas_call(
+        sum_x_kernel,
+        out_shape=jax.ShapeDtypeStruct((NZ, NP + GT, ROWS, BLK), jnp.float32),
+        in_specs=[pl.BlockSpec(memory_space=pltpu.SMEM), vmem, vmem],
         out_specs=vmem,
         compiler_params=params(),
-        name="pack",
-    )(first, factor)
-
-
-def sum_x_kernel(a_ref, b_ref, c_ref, d_ref, o_ref):
-    o_ref[...] = (a_ref[...] + b_ref[...]) + (c_ref[...] + d_ref[...])
-
-
-def sum_x(parts):
-    vmem = pl.BlockSpec(memory_space=pltpu.VMEM)
-    return pl.pallas_call(
-        sum_x_kernel,
-        out_shape=jax.ShapeDtypeStruct((NZ, GT, ROWS, BLK), jnp.float32),
-        in_specs=[vmem] * NX,
-        out_specs=vmem,
-        compiler_params=params(),
         name="sum_x",
-    )(*parts)
+    )(first, factor, received)
 
 
 def sum_z_kernel(g_ref, own_ref, o_ref):
-    total = g_ref[0]
+    total = g_ref[0, NP:]
     for i in range(1, NZ):
-        total = total + g_ref[i]
+        total = total + g_ref[i, NP:]
     own_ref[...] = total
     for d in range(DP):
         o_ref[d] = total
@@ -416,20 +401,17 @@
     tokens = token_ids.reshape(1, -1)
     x = lax.axis_index("x").reshape(1).astype(jnp.int32)
     first = (lax.axis_index(dp) * ROWS).reshape(1).astype(jnp.int32)
-    packed = pack(first, inv_chol)
-    mine = exchange(packed, "z")
-    partial = gram_partial(x, tokens, activations)
-    parts = [near(partial[0])]
-    for off in range(1, NX):
-        parts.append(near(shift_x(partial[off], off)))
-    rows = sum_x(parts)
-    mine, rows = lax.optimization_barrier((mine, rows))
-    rows = exchange(rows, "z")
+    partial = gram_partial(tokens, activations)
+    rows = exchange(partial, "x")
+    grams, diagonals = error_grams(weight)
+    packed = sum_x(first, near(inv_chol), near(rows))
+    over_z = exchange(packed, "z")
+    own, copies = sum_z(near(over_z))
+    gram = exchange(copies, dp)
+    mine, _ = lax.optimization_barrier((over_z, copies))
+    mine = mine[:, :NP]
     left = shift_x(mine, 1)
     right = shift_x(mine, -1)
-    own, copies = sum_z(near(rows))
-    gram = exchange(copies, dp)
-    grams, diagonals = error_grams(weight)
     row = scores(tokens, near(gram), near(grams), diagonals)
     left_late, _ = lax.optimization_barrier((left, row))
     row = exchange(row, dp)

time: 120 us -> 115 us (0.958)
  starting transfers between devices: 43 us -> 26.4 us
  blocking collectives: 35 us -> 45.9 us
  waiting for transfers between devices: 10.7 us -> 14 us
  Pallas kernels: 27.5 us -> 25.9 us
    all_to_all x2, blocking collectives: 35 us -> 45.9 us  [exchange(): return lax.all_to_all(pieces, axes, 0, 0, tiled=False)]
    ppermute x6 -> x3, starting transfers between devices: 18.9 us -> 8.4 us  [shift_x(): return lax.ppermute(piece, 'x', [(i, (i + by) % NX) for i in range(NX)])]
    all_to_all x3, starting transfers between devices: 24.1 us -> 18 us  [exchange(): return lax.all_to_all(pieces, axes, 0, 0, tiled=False)]
    all_to_all x3, waiting for transfers between devices: 8.09 us -> 14 us  [exchange(): return lax.all_to_all(pieces, axes, 0, 0, tiled=False)]
    ppermute x6 -> x3, waiting for transfers between devices: 2.62 us -> 0.01 us  [shift_x(): return lax.ppermute(piece, 'x', [(i, (i + by) % NX) for i in range(NX)])]
    pallas_call x3 -> x2, Pallas kernels: 4.98 us -> 3.44 us  [the longest x1 2.54 us: gram_partial(): pl.pallas_call(gram_kernel, out_shape=pltpu.VMEM((NX, NZ, GT, ROWS, BLK),...]
  transfers between devices with their start and end apart: 9 -> 6, of which waited for: 2 -> 2; matrix products, arithmetic and copies ran while one was open for 0% -> 0% of each run, Pallas kernels for 16% -> 13%
where the time goes in v1:
time: 115 us
  blocking collectives  45.9 us (40%)
  starting transfers between devices  26.4 us (23%)
  Pallas kernels  25.9 us (23%)
  waiting for transfers between devices  14 us (12%)
  local copies, waits for them, and re-layouts  1.62 us (1%)
    all_to_all x2, blocking collectives, exchange(): return lax.all_to_all(pieces, axes, 0, 0, tiled=False)  45.9 us
    all_to_all x3, starting transfers between devices, exchange(): return lax.all_to_all(pieces, axes, 0, 0, tiled=False)  18 us
    all_to_all x3, waiting for transfers between devices, exchange(): return lax.all_to_all(pieces, axes, 0, 0, tiled=False)  14 us
    pallas_call x1, Pallas kernels, error_grams(): pl.pallas_call(error_kernel, out_shape=(jax.ShapeDtypeStruct((NB, 4, DP,...  11.2 us
    ppermute x3, starting transfers between devices, shift_x(): return lax.ppermute(piece, 'x', [(i, (i + by) % NX) for i in range(NX)])  8.4 us
    pallas_call x1, Pallas kernels, quantize(): pl.pallas_call(quant_kernel, out_shape=jax.ShapeDtypeStruct((rows, PANEL)...  6.43 us
    pallas_call x1, Pallas kernels, gram_partial(): pl.pallas_call(gram_kernel, out_shape=pltpu.VMEM((NX, NZ, GT, ROWS, BLK),...  2.54 us
  transfers between devices with their start and end apart: 6, of which 2 were waited for; matrix products, arithmetic and copies ran while one was open for 0% of the time, Pallas kernels for 13%

profile of v1, /device:TPU:1, one launch (start us, length us, event | category | flops | bytes accessed | tf_op | source)
XLA Modules:
  0.0 114.6 jit_solution(12948747080725806727)
XLA Ops:
  0.6 0.0 copy-start.1
  0.6 2.5 %gram_partial.1 = f32[4,8,5,4,128]{4,3,2,1,0:T(4,128)} custom-call(s32[1,512]{1,0:T(1,128)} %bitcast.4, bf16[512,1024]{1,0:T(8,128)(2,1)} %a_ref.1), custom_call_target="tpu_custom_call" | custom-call | tf_op jit(solution)/shard_map/gram_partial/pallas_call | solution.py:70
  3.2 4.8 %all-to-all-start = ((f32[4,8,5,4,128]{4,3,2,1,0:T(4,128)}), f32[4,8,5,4,128]{4,3,2,1,0:T(4,128)S(1)}, u32[]{:S(2)}, u32[]{:S(2)}) async-start(f32[4,8,5,4,128]{4,3,2,1,0:T(4,128)} %gram_partial.1), calls=%async_computation | async-start | bytes 655360 | tf_op jit(solution)/shard_map/all_to_all | solution.py:387
  8.0 5.9 %all-to-all-done.g_ref = f32[4,8,5,4,128]{4,3,2,1,0:T(4,128)S(1)} async-done(((f32[4,8,5,4,128]{4,3,2,1,0:T(4,128)}), f32[4,8,5,4,128]{4,3,2,1,0:T(4,128)S(1)}, u32[]{:S(2)}, u32[]{:S(2)}) %all-to-all-start) | async-done | bytes 327712 | tf_op jit(solution)/shard_map/all_to_all | solution.py:387
  13.9 0.0 copy-done.1
  13.9 0.9 sum_x.1
  14.8 25.6 %all_to_all.25.g_ref = f32[8,34,4,128]{3,2,1,0:T(4,128)S(1)} all-to-all(f32[8,34,4,128]{3,2,1,0:T(4,128)} %sum_x.1), channel_id=1, replica_groups=mesh['x'=4,'z'=8,'y'=8,'c'=2] {'z'}, dimensions={0} | all-to-all | bytes 1114112 | tf_op jit(solution)/shard_map/all_to_all | solution.py:387
  40.4 0.8 sum_z.1
  41.2 4.0 %all-to-all-start.2 = ((f32[32,5,4,128]{3,2,1,0:T(4,128)}), f32[32,5,4,128]{3,2,1,0:T(4,128)S(1)}, u32[]{:S(2)}, u32[]{:S(2)}) async-start(f32[32,5,4,128]{3,2,1,0:T(4,128)} %get-tuple-element.11), calls=%async_computation.2 | async-start | bytes 655360 | tf_op jit(solution)/shard_map/all_to_all | solution.py:387
  45.2 3.1 %collective-permute-start = (f32[8,29,4,128]{3,2,1,0:T(4,128)S(1)}, f32[8,29,4,128]{3,2,1,0:T(4,128)S(1)}, u32[]{:S(2)}, u32[]{:S(2)}) collective-permute-start(f32[8,29,4,128]{3,2,1,0:T(4,128)S(1)} %slice.3.own_ref), channel_id=1, source_target_pairs={{0,128},{128,256},{256,384},{384,0},{1,129},{129,257},{257,385},{3... | collective-permute-start | bytes 1425416 | tf_op jit(solution)/shard_map/ppermute | solution.py:391
  48.4 11.2 %error_grams.1 = (f32[8,4,32,4,128]{4,3,2,1,0:T(4,128)}, f32[4,32,4,128]{3,2,1,0:T(4,128)}) custom-call(bf16[512,1024]{1,0:T(8,128)(2,1)} %w_ref.3), custom_call_target="tpu_custom_call" | custom-call | tf_op jit(solution)/shard_map/error_grams/pallas_call | solution.py:165
  59.5 3.3 %collective-permute-start.1 = (f32[8,29,4,128]{3,2,1,0:T(4,128)S(1)}, f32[8,29,4,128]{3,2,1,0:T(4,128)S(1)}, u32[]{:S(2)}, u32[]{:S(2)}) collective-permute-start(f32[8,29,4,128]{3,2,1,0:T(4,128)S(1)} %slice.3.own_ref), channel_id=1, source_target_pairs={{0,384},{128,0},{256,128},{384,256},{1,385},{129,1},{257,129},{385... | collective-permute-start | bytes 1425416 | tf_op jit(solution)/shard_map/ppermute | solution.py:391
  62.9 0.0 all-to-all-done.2.g_ref
  62.9 0.0 copy-start
  62.9 1.6 %copy-done = f32[8,4,32,4,128]{4,3,2,1,0:T(4,128)S(1)} copy-done((f32[8,4,32,4,128]{4,3,2,1,0:T(4,128)S(1)}, f32[8,4,32,4,128]{4,3,2,1,0:T(4,128)}, u32[]{:S(2)}) %copy-start) | copy-done | bytes 2097176
  64.5 2.1 %scores.1 = f32[32,1,128]{2,1,0:T(1,128)} custom-call(s32[1,512]{1,0:T(1,128)} %bitcast.5, f32[32,5,4,128]{3,2,1,0:T(4,128)S(1)} %all-to-all-done.2.g_ref, f32[8,4,32,4,128]{4,3,2,1,0:T(4,128)S(1)} %copy-done, f32[4,32,4,128]{3,2,1,0:T(4,128)} %get-tuple-element.14.d_ref), custom_call_target="tpu_custom_call" | custom-call | tf_op jit(solution)/shard_map/scores/pallas_call | solution.py:205
  66.6 0.0 collective-permute-done.left_ref
  66.6 1.9 %collective-permute-start.2 = (f32[8,29,4,128]{3,2,1,0:T(4,128)S(1)}, f32[8,29,4,128]{3,2,1,0:T(4,128)S(1)}, u32[]{:S(2)}, u32[]{:S(2)}) collective-permute-start(f32[8,29,4,128]{3,2,1,0:T(4,128)S(1)} %collective-permute-done.left_ref), channel_id=1, source_target_pairs={{0,128},{128,256},{256,384},{384,0},{1,129},{129,257},{257,385},{3... | collective-permute-start | bytes 1425416 | tf_op jit(solution)/shard_map/ppermute | solution.py:391
  68.5 9.2 %all-to-all-start.3 = ((f32[32,1,128]{2,1,0:T(1,128)}), f32[32,1,128]{2,1,0:T(1,128)S(1)}, u32[]{:S(2)}, u32[]{:S(2)}) async-start(f32[32,1,128]{2,1,0:T(1,128)} %scores.1), calls=%async_computation.3 | async-start | bytes 32768 | tf_op jit(solution)/shard_map/all_to_all | solution.py:387
  77.7 0.5 gram_rows.1.own_ref
  78.2 8.1 %all-to-all-done.3.r_ref = f32[32,1,128]{2,1,0:T(1,128)S(1)} async-done(((f32[32,1,128]{2,1,0:T(1,128)}), f32[32,1,128]{2,1,0:T(1,128)S(1)}, u32[]{:S(2)}, u32[]{:S(2)}) %all-to-all-start.3) | async-done | bytes 16416 | tf_op jit(solution)/shard_map/all_to_all | solution.py:387
  86.3 0.8 totals.1
  87.1 20.3 %all_to_all.26.r_ref = f32[16,1,128]{2,1,0:T(1,128)S(1)} all-to-all(f32[16,1,128]{2,1,0:T(1,128)} %get-tuple-element.18), channel_id=1, replica_groups=mesh['x'=4,'z'=8,'y'=8,'c'=2] {'y','c'}, dimensions={0} | all-to-all | bytes 16384 | tf_op jit(solution)/shard_map/all_to_all | solution.py:387
  107.4 0.7 spread.1
  108.1 0.0 collective-permute-done.1.right_ref
  108.1 0.0 collective-permute-done.2.far_ref
  108.1 6.4 %quantize.1 = bf16[512,1024]{1,0:T(8,128)(2,1)} custom-call(s32[8]{0:T(128)} %bits_ref.1, s32[1]{0:T(128)} %bitcast.x_ref, bf16[512,1024]{1,0:T(8,128)(2,1)} %w_ref.3, f32[8,29,4,128]{3,2,1,0:T(4,128)S(1)} %slice.3.own_ref, f32[8,29,4,128]{3,2,1,0:T(4,128)S(1)} %collective-permute-done.left_ref, f32[8,29,4,128]{3,2,1,0:T(4,128)S(1)} %collective-permute-done.1.right_ref, ...), custom_call_target="tpu_custom_call" | custom-call | tf_op jit(solution)/shard_map/quantize/pallas_call | solution.py:367
  (1 shorter events, 0.0 us)
Async XLA Ops:
  0.6 13.3 %copy-start.1 = (f32[8,4,1024]{2,1,0:T(4,128)S(1)}, f32[8,4,1024]{2,1,0:T(4,128)}, u32[]{:S(2)}) copy-start(f32[8,4,1024]{2,1,0:T(4,128)} %f_ref.1) | copy-start | bytes 393220
  3.2 10.7 %all-to-all-start = ((f32[4,8,5,4,128]{4,3,2,1,0:T(4,128)}), f32[4,8,5,4,128]{4,3,2,1,0:T(4,128)S(1)}, u32[]{:S(2)}, u32[]{:S(2)}) async-start(f32[4,8,5,4,128]{4,3,2,1,0:T(4,128)} %gram_partial.1), calls=%async_computation | async-start | bytes 655360 | tf_op jit(solution)/shard_map/all_to_all | solution.py:387
  41.2 21.7 %all-to-all-start.2 = ((f32[32,5,4,128]{3,2,1,0:T(4,128)}), f32[32,5,4,128]{3,2,1,0:T(4,128)S(1)}, u32[]{:S(2)}, u32[]{:S(2)}) async-start(f32[32,5,4,128]{3,2,1,0:T(4,128)} %get-tuple-element.11), calls=%async_computation.2 | async-start | bytes 655360 | tf_op jit(solution)/shard_map/all_to_all | solution.py:387
  45.2 21.4 %collective-permute-start = (f32[8,29,4,128]{3,2,1,0:T(4,128)S(1)}, f32[8,29,4,128]{3,2,1,0:T(4,128)S(1)}, u32[]{:S(2)}, u32[]{:S(2)}) collective-permute-start(f32[8,29,4,128]{3,2,1,0:T(4,128)S(1)} %slice.3.own_ref), channel_id=1, source_target_pairs={{0,128},{128,256},{256,384},{384,0},{1,129},{129,257},{257,385},{3... | collective-permute-start | bytes 1425416 | tf_op jit(solution)/shard_map/ppermute | solution.py:391
  59.5 48.6 %collective-permute-start.1 = (f32[8,29,4,128]{3,2,1,0:T(4,128)S(1)}, f32[8,29,4,128]{3,2,1,0:T(4,128)S(1)}, u32[]{:S(2)}, u32[]{:S(2)}) collective-permute-start(f32[8,29,4,128]{3,2,1,0:T(4,128)S(1)} %slice.3.own_ref), channel_id=1, source_target_pairs={{0,384},{128,0},{256,128},{384,256},{1,385},{129,1},{257,129},{385... | collective-permute-start | bytes 1425416 | tf_op jit(solution)/shard_map/ppermute | solution.py:391
  62.9 1.6 %copy-start = (f32[8,4,32,4,128]{4,3,2,1,0:T(4,128)S(1)}, f32[8,4,32,4,128]{4,3,2,1,0:T(4,128)}, u32[]{:S(2)}) copy-start(f32[8,4,32,4,128]{4,3,2,1,0:T(4,128)} %get-tuple-element.13.s_ref) | copy-start | bytes 6291460
  66.6 41.6 %collective-permute-start.2 = (f32[8,29,4,128]{3,2,1,0:T(4,128)S(1)}, f32[8,29,4,128]{3,2,1,0:T(4,128)S(1)}, u32[]{:S(2)}, u32[]{:S(2)}) collective-permute-start(f32[8,29,4,128]{3,2,1,0:T(4,128)S(1)} %collective-permute-done.left_ref), channel_id=1, source_target_pairs={{0,128},{128,256},{256,384},{384,0},{1,129},{129,257},{257,385},{3... | collective-permute-start | bytes 1425416 | tf_op jit(solution)/shard_map/ppermute | solution.py:391
  68.5 17.8 %all-to-all-start.3 = ((f32[32,1,128]{2,1,0:T(1,128)}), f32[32,1,128]{2,1,0:T(1,128)S(1)}, u32[]{:S(2)}, u32[]{:S(2)}) async-start(f32[32,1,128]{2,1,0:T(1,128)} %scores.1), calls=%async_computation.3 | async-start | bytes 32768 | tf_op jit(solution)/shard_map/all_to_all | solution.py:387

commit v2 on v1

--- a/solution.py
+++ b/solution.py
@@ -17,6 +17,7 @@
 NP = len(PAIRS) + 1
 HB = NB // 2
 GT = HB + 1
+DL = NB
 PAD = 128004
 LEVELS = (2.0, 4.0, 8.0, 128.0)
 
@@ -61,7 +62,7 @@
         lower = gram(b + HB)
         put(jnp.where(col >= row, gram(b), lower), b)
         value = jnp.sum(jnp.where(col == row, lower, 0.0), axis=1, keepdims=True)
-        diag = jnp.where(col == b + HB, value, diag)
+        diag = jnp.where(col == DL + b + HB, value, diag)
     put(diag, HB)
 
 
@@ -86,8 +87,6 @@
         tile = f_ref[j, :, j * BLK : (j + 1) * BLK]
         value = jnp.sum(jnp.where(on_diag, tile, 0.0), axis=1, keepdims=True)
         diag = jnp.where(lane == j, value, diag)
-    for i in range(NZ):
-        o_ref[i, NP - 1] = diag
     for p, (j, c) in enumerate(PAIRS):
         tile = f_ref[j, :, c * BLK : (c + 1) * BLK]
         for i in range(NZ):
@@ -96,14 +95,15 @@
         total = g_ref[0, i]
         for x in range(1, NX):
             total = total + g_ref[x, i]
-        o_ref[i, NP:] = total
+        o_ref[i, NP:] = total[:HB]
+        o_ref[i, NP - 1] = diag + total[HB]
 
 
 def sum_x(first, factor, received):
     vmem = pl.BlockSpec(memory_space=pltpu.VMEM)
     return pl.pallas_call(
         sum_x_kernel,
-        out_shape=jax.ShapeDtypeStruct((NZ, NP + GT, ROWS, BLK), jnp.float32),
+        out_shape=jax.ShapeDtypeStruct((NZ, NP + HB, ROWS, BLK), jnp.float32),
         in_specs=[pl.BlockSpec(memory_space=pltpu.SMEM), vmem, vmem],
         out_specs=vmem,
         compiler_params=params(),
@@ -112,12 +112,16 @@
 
 
 def sum_z_kernel(g_ref, own_ref, o_ref):
-    total = g_ref[0, NP:]
+    total = g_ref[0, NP - 1 :]
     for i in range(1, NZ):
-        total = total + g_ref[i, NP:]
-    own_ref[...] = total
+        total = total + g_ref[i, NP - 1 :]
+    lane = lax.broadcasted_iota(jnp.int32, (ROWS, BLK), 1)
+    diag = jnp.where(lane >= DL, total[0], 0.0)
+    own_ref[:HB] = total[1:]
+    own_ref[HB] = diag
     for d in range(DP):
-        o_ref[d] = total
+        o_ref[d, :HB] = total[1:]
+        o_ref[d, HB] = diag
 
 
 def sum_z(received):
@@ -151,7 +155,7 @@
         e = (w - (bound * (1.0 / (levels - 0.5))) * smooth).astype(jnp.bfloat16)
         s = lax.dot_general(e, e, (((0,), (0,)), ((), ())), preferred_element_type=jnp.float32)
         value = jnp.sum(jnp.where(col == row, s, 0.0), axis=1, keepdims=True)
-        diag = jnp.where((col == b) & (b >= HB), value, 0.0)
+        diag = jnp.where((col == DL + b) & (b >= HB), value, 0.0)
         s = s * weight
         for d in range(DP):
             part = slice(d * ROWS, (d + 1) * ROWS)
@@ -194,7 +198,7 @@
         for d in range(1, DP):
             acc = acc + g_ref[d, HB] * d_ref[k, d]
         acc = jnp.sum(acc, axis=0, keepdims=True)
-        diagonals = diagonals + (pltpu.roll(acc, k * NB, 1) if k else acc)
+        diagonals = diagonals + (acc if k * NB == DL else pltpu.roll(acc, (k * NB - DL) % BLK, 1))
     row = jnp.sum(row_ref[...].T, axis=0, keepdims=True) + diagonals
     for d in range(DP):
         o_ref[d] = row
@@ -230,7 +234,7 @@
             preferred_element_type=jnp.float32,
         )[:ROWS]
         own = own_ref[b]
-        diag = jnp.sum(jnp.where(lane == b + HB, own_ref[HB], 0.0), axis=1, keepdims=True)
+        diag = jnp.sum(jnp.where(lane == DL + b + HB, own_ref[HB], 0.0), axis=1, keepdims=True)
         o_ref[b] = jnp.where(lane >= mine, own, turned)
         o_ref[b + HB] = jnp.where(lane < mine, own, jnp.where(lane == mine, diag, turned))
 

time: 115 us -> 115 us (level)
  no operation moved by 1% of the time
where the time goes in v2:
time: 115 us; the launch traced here: 114 us
  blocking collectives  45 us (39%)
  starting transfers between devices  26.9 us (23%)
  Pallas kernels  25.9 us (23%)
  waiting for transfers between devices  14 us (12%)
  local copies, waits for them, and re-layouts  1.62 us (1%)
    all_to_all x2, blocking collectives, exchange(): return lax.all_to_all(pieces, axes, 0, 0, tiled=False)  45 us
    all_to_all x3, starting transfers between devices, exchange(): return lax.all_to_all(pieces, axes, 0, 0, tiled=False)  18.5 us
    all_to_all x3, waiting for transfers between devices, exchange(): return lax.all_to_all(pieces, axes, 0, 0, tiled=False)  14 us
    pallas_call x1, Pallas kernels, error_grams(): pl.pallas_call(error_kernel, out_shape=(jax.ShapeDtypeStruct((NB, 4, DP,...  11.2 us
    ppermute x3, starting transfers between devices, shift_x(): return lax.ppermute(piece, 'x', [(i, (i + by) % NX) for i in range(NX)])  8.4 us
    pallas_call x1, Pallas kernels, quantize(): pl.pallas_call(quant_kernel, out_shape=jax.ShapeDtypeStruct((rows, PANEL)...  6.43 us
    pallas_call x1, Pallas kernels, gram_partial(): pl.pallas_call(gram_kernel, out_shape=pltpu.VMEM((NX, NZ, GT, ROWS, BLK),...  2.54 us
  transfers between devices with their start and end apart: 6, of which 2 were waited for; matrix products, arithmetic and copies ran while one was open for 0% of the time, Pallas kernels for 13%

profile of v2, /device:TPU:1, one launch (start us, length us, event | category | flops | bytes accessed | tf_op | source)
XLA Modules:
  0.0 114.2 jit_solution(5300495787935046070)
XLA Ops:
  0.6 0.0 copy-start.1
  0.6 2.5 %gram_partial.1 = f32[4,8,5,4,128]{4,3,2,1,0:T(4,128)} custom-call(s32[1,512]{1,0:T(1,128)} %bitcast.4, bf16[512,1024]{1,0:T(8,128)(2,1)} %a_ref.1), custom_call_target="tpu_custom_call" | custom-call | tf_op jit(solution)/shard_map/gram_partial/pallas_call | solution.py:71
  3.2 4.8 %all-to-all-start = ((f32[4,8,5,4,128]{4,3,2,1,0:T(4,128)}), f32[4,8,5,4,128]{4,3,2,1,0:T(4,128)S(1)}, u32[]{:S(2)}, u32[]{:S(2)}) async-start(f32[4,8,5,4,128]{4,3,2,1,0:T(4,128)} %gram_partial.1), calls=%async_computation | async-start | bytes 655360 | tf_op jit(solution)/shard_map/all_to_all | solution.py:391
  8.0 5.9 %all-to-all-done.g_ref = f32[4,8,5,4,128]{4,3,2,1,0:T(4,128)S(1)} async-done(((f32[4,8,5,4,128]{4,3,2,1,0:T(4,128)}), f32[4,8,5,4,128]{4,3,2,1,0:T(4,128)S(1)}, u32[]{:S(2)}, u32[]{:S(2)}) %all-to-all-start) | async-done | bytes 327712 | tf_op jit(solution)/shard_map/all_to_all | solution.py:391
  13.9 0.0 copy-done.1
  13.9 0.9 sum_x.1
  14.8 25.0 %all_to_all.25.g_ref = f32[8,33,4,128]{3,2,1,0:T(4,128)S(1)} all-to-all(f32[8,33,4,128]{3,2,1,0:T(4,128)} %sum_x.1), channel_id=1, replica_groups=mesh['x'=4,'z'=8,'y'=8,'c'=2] {'z'}, dimensions={0} | all-to-all | bytes 1081344 | tf_op jit(solution)/shard_map/all_to_all | solution.py:391
  39.8 0.8 sum_z.1
  40.6 4.5 %all-to-all-start.2 = ((f32[32,5,4,128]{3,2,1,0:T(4,128)}), f32[32,5,4,128]{3,2,1,0:T(4,128)S(1)}, u32[]{:S(2)}, u32[]{:S(2)}) async-start(f32[32,5,4,128]{3,2,1,0:T(4,128)} %get-tuple-element.11), calls=%async_computation.2 | async-start | bytes 655360 | tf_op jit(solution)/shard_map/all_to_all | solution.py:391
  45.1 3.1 %collective-permute-start = (f32[8,29,4,128]{3,2,1,0:T(4,128)S(1)}, f32[8,29,4,128]{3,2,1,0:T(4,128)S(1)}, u32[]{:S(2)}, u32[]{:S(2)}) collective-permute-start(f32[8,29,4,128]{3,2,1,0:T(4,128)S(1)} %slice.3.own_ref), channel_id=1, source_target_pairs={{0,128},{128,256},{256,384},{384,0},{1,129},{129,257},{257,385},{3... | collective-permute-start | bytes 1425416 | tf_op jit(solution)/shard_map/ppermute | solution.py:395
  48.3 11.2 %error_grams.1 = (f32[8,4,32,4,128]{4,3,2,1,0:T(4,128)}, f32[4,32,4,128]{3,2,1,0:T(4,128)}) custom-call(bf16[512,1024]{1,0:T(8,128)(2,1)} %w_ref.3), custom_call_target="tpu_custom_call" | custom-call | tf_op jit(solution)/shard_map/error_grams/pallas_call | solution.py:169
  59.5 3.3 %collective-permute-start.1 = (f32[8,29,4,128]{3,2,1,0:T(4,128)S(1)}, f32[8,29,4,128]{3,2,1,0:T(4,128)S(1)}, u32[]{:S(2)}, u32[]{:S(2)}) collective-permute-start(f32[8,29,4,128]{3,2,1,0:T(4,128)S(1)} %slice.3.own_ref), channel_id=1, source_target_pairs={{0,384},{128,0},{256,128},{384,256},{1,385},{129,1},{257,129},{385... | collective-permute-start | bytes 1425416 | tf_op jit(solution)/shard_map/ppermute | solution.py:395
  62.8 0.0 all-to-all-done.2.g_ref
  62.8 0.0 copy-start
  62.8 1.6 %copy-done = f32[8,4,32,4,128]{4,3,2,1,0:T(4,128)S(1)} copy-done((f32[8,4,32,4,128]{4,3,2,1,0:T(4,128)S(1)}, f32[8,4,32,4,128]{4,3,2,1,0:T(4,128)}, u32[]{:S(2)}) %copy-start) | copy-done | bytes 2097176
  64.4 2.1 %scores.1 = f32[32,1,128]{2,1,0:T(1,128)} custom-call(s32[1,512]{1,0:T(1,128)} %bitcast.5, f32[32,5,4,128]{3,2,1,0:T(4,128)S(1)} %all-to-all-done.2.g_ref, f32[8,4,32,4,128]{4,3,2,1,0:T(4,128)S(1)} %copy-done, f32[4,32,4,128]{3,2,1,0:T(4,128)} %get-tuple-element.14.d_ref), custom_call_target="tpu_custom_call" | custom-call | tf_op jit(solution)/shard_map/scores/pallas_call | solution.py:209
  66.5 0.0 collective-permute-done.left_ref
  66.5 1.9 %collective-permute-start.2 = (f32[8,29,4,128]{3,2,1,0:T(4,128)S(1)}, f32[8,29,4,128]{3,2,1,0:T(4,128)S(1)}, u32[]{:S(2)}, u32[]{:S(2)}) collective-permute-start(f32[8,29,4,128]{3,2,1,0:T(4,128)S(1)} %collective-permute-done.left_ref), channel_id=1, source_target_pairs={{0,128},{128,256},{256,384},{384,0},{1,129},{129,257},{257,385},{3... | collective-permute-start | bytes 1425416 | tf_op jit(solution)/shard_map/ppermute | solution.py:395
  68.4 9.2 %all-to-all-start.3 = ((f32[32,1,128]{2,1,0:T(1,128)}), f32[32,1,128]{2,1,0:T(1,128)S(1)}, u32[]{:S(2)}, u32[]{:S(2)}) async-start(f32[32,1,128]{2,1,0:T(1,128)} %scores.1), calls=%async_computation.3 | async-start | bytes 32768 | tf_op jit(solution)/shard_map/all_to_all | solution.py:391
  77.6 0.5 gram_rows.1.own_ref
  78.1 8.1 %all-to-all-done.3.r_ref = f32[32,1,128]{2,1,0:T(1,128)S(1)} async-done(((f32[32,1,128]{2,1,0:T(1,128)}), f32[32,1,128]{2,1,0:T(1,128)S(1)}, u32[]{:S(2)}, u32[]{:S(2)}) %all-to-all-start.3) | async-done | bytes 16416 | tf_op jit(solution)/shard_map/all_to_all | solution.py:391
  86.2 0.8 totals.1
  87.0 20.0 %all_to_all.26.r_ref = f32[16,1,128]{2,1,0:T(1,128)S(1)} all-to-all(f32[16,1,128]{2,1,0:T(1,128)} %get-tuple-element.18), channel_id=1, replica_groups=mesh['x'=4,'z'=8,'y'=8,'c'=2] {'y','c'}, dimensions={0} | all-to-all | bytes 16384 | tf_op jit(solution)/shard_map/all_to_all | solution.py:391
  107.0 0.7 spread.1
  107.8 0.0 collective-permute-done.1.right_ref
  107.8 0.0 collective-permute-done.2.far_ref
  107.8 6.4 %quantize.1 = bf16[512,1024]{1,0:T(8,128)(2,1)} custom-call(s32[8]{0:T(128)} %bits_ref.1, s32[1]{0:T(128)} %bitcast.x_ref, bf16[512,1024]{1,0:T(8,128)(2,1)} %w_ref.3, f32[8,29,4,128]{3,2,1,0:T(4,128)S(1)} %slice.3.own_ref, f32[8,29,4,128]{3,2,1,0:T(4,128)S(1)} %collective-permute-done.left_ref, f32[8,29,4,128]{3,2,1,0:T(4,128)S(1)} %collective-permute-done.1.right_ref, ...), custom_call_target="tpu_custom_call" | custom-call | tf_op jit(solution)/shard_map/quantize/pallas_call | solution.py:371
  (1 shorter events, 0.0 us)
Async XLA Ops:
  0.6 13.3 %copy-start.1 = (f32[8,4,1024]{2,1,0:T(4,128)S(1)}, f32[8,4,1024]{2,1,0:T(4,128)}, u32[]{:S(2)}) copy-start(f32[8,4,1024]{2,1,0:T(4,128)} %f_ref.1) | copy-start | bytes 393220
  3.2 10.7 %all-to-all-start = ((f32[4,8,5,4,128]{4,3,2,1,0:T(4,128)}), f32[4,8,5,4,128]{4,3,2,1,0:T(4,128)S(1)}, u32[]{:S(2)}, u32[]{:S(2)}) async-start(f32[4,8,5,4,128]{4,3,2,1,0:T(4,128)} %gram_partial.1), calls=%async_computation | async-start | bytes 655360 | tf_op jit(solution)/shard_map/all_to_all | solution.py:391
  40.6 22.2 %all-to-all-start.2 = ((f32[32,5,4,128]{3,2,1,0:T(4,128)}), f32[32,5,4,128]{3,2,1,0:T(4,128)S(1)}, u32[]{:S(2)}, u32[]{:S(2)}) async-start(f32[32,5,4,128]{3,2,1,0:T(4,128)} %get-tuple-element.11), calls=%async_computation.2 | async-start | bytes 655360 | tf_op jit(solution)/shard_map/all_to_all | solution.py:391
  45.1 21.4 %collective-permute-start = (f32[8,29,4,128]{3,2,1,0:T(4,128)S(1)}, f32[8,29,4,128]{3,2,1,0:T(4,128)S(1)}, u32[]{:S(2)}, u32[]{:S(2)}) collective-permute-start(f32[8,29,4,128]{3,2,1,0:T(4,128)S(1)} %slice.3.own_ref), channel_id=1, source_target_pairs={{0,128},{128,256},{256,384},{384,0},{1,129},{129,257},{257,385},{3... | collective-permute-start | bytes 1425416 | tf_op jit(solution)/shard_map/ppermute | solution.py:395
  59.5 48.3 %collective-permute-start.1 = (f32[8,29,4,128]{3,2,1,0:T(4,128)S(1)}, f32[8,29,4,128]{3,2,1,0:T(4,128)S(1)}, u32[]{:S(2)}, u32[]{:S(2)}) collective-permute-start(f32[8,29,4,128]{3,2,1,0:T(4,128)S(1)} %slice.3.own_ref), channel_id=1, source_target_pairs={{0,384},{128,0},{256,128},{384,256},{1,385},{129,1},{257,129},{385... | collective-permute-start | bytes 1425416 | tf_op jit(solution)/shard_map/ppermute | solution.py:395
  62.8 1.6 %copy-start = (f32[8,4,32,4,128]{4,3,2,1,0:T(4,128)S(1)}, f32[8,4,32,4,128]{4,3,2,1,0:T(4,128)}, u32[]{:S(2)}) copy-start(f32[8,4,32,4,128]{4,3,2,1,0:T(4,128)} %get-tuple-element.13.s_ref) | copy-start | bytes 6291460
  66.5 41.3 %collective-permute-start.2 = (f32[8,29,4,128]{3,2,1,0:T(4,128)S(1)}, f32[8,29,4,128]{3,2,1,0:T(4,128)S(1)}, u32[]{:S(2)}, u32[]{:S(2)}) collective-permute-start(f32[8,29,4,128]{3,2,1,0:T(4,128)S(1)} %collective-permute-done.left_ref), channel_id=1, source_target_pairs={{0,128},{128,256},{256,384},{384,0},{1,129},{129,257},{257,385},{3... | collective-permute-start | bytes 1425416 | tf_op jit(solution)/shard_map/ppermute | solution.py:395
  68.4 17.8 %all-to-all-start.3 = ((f32[32,1,128]{2,1,0:T(1,128)}), f32[32,1,128]{2,1,0:T(1,128)S(1)}, u32[]{:S(2)}, u32[]{:S(2)}) async-start(f32[32,1,128]{2,1,0:T(1,128)} %scores.1), calls=%async_computation.3 | async-start | bytes 32768 | tf_op jit(solution)/shard_map/all_to_all | solution.py:391
